TPU v7x, 256 devices: a whole 4x4x8 slice. The times are simulated.
256 devices in a mesh: dp: 16 (over z, core), expert: 16 (over y, x).
Axes of the slice: x: 4, y: 4, z: 8, core: 2. Of those that a mesh axis runs over, the one named last changes fastest.
Arguments:
- ssm_state: bfloat16 [1024, 16, 4096], P('expert', None, 'dp'), may hold values from -6 to 6
- conv_state: bfloat16 [1024, 3, 4096], P('expert', None, 'dp'), may hold values from -6 to 6
- new_slot: int32 [1024], replicated, may hold values from 0 to 1023, as said below
- conv_input: bfloat16 [1024, 4096], P('expert', 'dp'), may hold values from -6 to 6
- gate_input: bfloat16 [1024, 4096], P('expert', 'dp'), may hold values from -6 to 6
- conv_weight: float32 [4, 4096], P(None, 'dp'), may hold values from -3 to 3
- conv_bias: float32 [4096], P('dp'), may hold values from -3 to 3
- x_proj_weight: bfloat16 [4096, 288], P('dp'), may hold values from -0.09375 to 0.09375
- step_weight: bfloat16 [256, 4096], P(None, 'dp'), may hold values from -0.375 to 0.375
- step_bias: float32 [4096], P('dp'), may hold values from -3 to -0.5
- decay_log: float32 [16, 4096], P(None, 'dp'), may hold values from 0 to 2
- skip_gain: float32 [4096], P('dp'), may hold values from 0.5 to 1.5
- out_proj_weight: bfloat16 [4096, 4096], P('dp', 'expert'), may hold values from -0.09375 to 0.09375
- residual: bfloat16 [1024, 4096], P(None, 'expert'), may hold values from -6 to 6
- norm_gain: float32 [4096], replicated, may hold values from 0.1 to 1.9
- routes: int32 [1024, 2], replicated, may hold values from 0 to 15, all different within a row; in each aligned block of 64 rows (0 to 63, 64 to 127, ...) at most 20 rows name the same one
- gate_weight: float32 [1024, 2], replicated, may hold values from 0.1 to 0.9
- expert_gate: bfloat16 [16, 4096, 7168], P('expert', None, 'dp'), may hold values from -0.09375 to 0.09375
- expert_up: bfloat16 [16, 4096, 7168], P('expert', None, 'dp'), may hold values from -0.09375 to 0.09375
- expert_down: bfloat16 [16, 7168, 4096], P('expert', 'dp'), may hold values from -0.0625 to 0.0625
Outputs:
- ssm_new: bfloat16 [1024, 16, 4096], P('expert', None, 'dp')
- conv_new: bfloat16 [1024, 3, 4096], P('expert', None, 'dp')
- layer_out: bfloat16 [1024, 4096], P(None, 'expert')
Inputs may be any that keep to these rules, and one draw needn't show every extreme that they name: new_slot is a permutation of the 1024 slots; slot s belongs to expert index s // 64. Of the 64 old slots of one expert index, at most 8 get new slots of any one expert index, and exactly 8 those of some expert index; every expert index sends the same multiset of such counts. `routes`: each row names 2 different experts; within each aligned block of 64 rows (the rows of one expert index) no expert is named by more than 20 rows, a bound that some block reaches.
All inputs are finite; a program needn't handle non-finite values.
Results may differ from a plain program's by a relative error of at most 0.012.
Values may be sent and summed in bfloat16 or wider, within the bound.
A program may use at most 128 MiB of HBM per device.

v0:
```python
import jax
import jax.numpy as jnp
from jax import lax
from jax.sharding import PartitionSpec as P


def dp_total(values):
    return lax.psum(values, "dp")


def body(
    ssm_state,
    conv_state,
    new_slot,
    conv_input,
    gate_input,
    conv_weight,
    conv_bias,
    x_proj_weight,
    step_weight,
    step_bias,
    decay_log,
    skip_gain,
    out_proj_weight,
    residual,
    norm_gain,
    routes,
    gate_weight,
    expert_gate,
    expert_up,
    expert_down,
):
    row_count, state_dim, channels = ssm_state.shape
    owners = lax.axis_size("expert")
    own_index = lax.axis_index("expert")
    move_cap = 2 * row_count // owners
    slot_count = owners * move_cap
    my_slots = lax.dynamic_slice_in_dim(new_slot, own_index * row_count, row_count)
    target = my_slots // row_count
    target_hot = (target[:, None] == jnp.arange(owners)[None, :]).astype(jnp.int32)
    earlier = jnp.sum((jnp.cumsum(target_hot, axis=0) - target_hot) * target_hot, axis=1)
    send_slot = target * move_cap + earlier
    send_hot = (jnp.arange(slot_count)[:, None] == send_slot[None, :]).astype(jnp.bfloat16)
    packed_ssm = (
        jnp.dot(send_hot, ssm_state.reshape(row_count, -1), preferred_element_type=jnp.float32)
        .astype(jnp.bfloat16)
        .reshape(owners, move_cap, -1)
    )
    packed_conv = (
        jnp.dot(send_hot, conv_state.reshape(row_count, -1), preferred_element_type=jnp.float32)
        .astype(jnp.bfloat16)
        .reshape(owners, move_cap, -1)
    )
    recv_ssm, recv_conv = (
        lax.all_to_all(packed_ssm, "expert", split_axis=0, concat_axis=0, tiled=True),
        lax.all_to_all(packed_conv, "expert", split_axis=0, concat_axis=0, tiled=True),
    )
    arriving = (new_slot // row_count == own_index).astype(jnp.int32).reshape(owners, row_count)
    arrive_rank = (jnp.cumsum(arriving, axis=1) - arriving).reshape(-1)
    source_ids = jnp.arange(owners * row_count) // row_count
    recv_slot = source_ids * move_cap + arrive_rank
    new_place = new_slot % row_count
    place_rows = (
        (new_place[None, :] == jnp.arange(row_count)[:, None])
        & (arriving.reshape(-1)[None, :] == 1)
    ).astype(jnp.bfloat16)
    place_slots = (recv_slot[:, None] == jnp.arange(slot_count)[None, :]).astype(jnp.bfloat16)
    place_hot = jnp.dot(place_rows, place_slots, preferred_element_type=jnp.float32).astype(
        jnp.bfloat16
    )
    moved_ssm = (
        jnp.dot(place_hot, recv_ssm.reshape(slot_count, -1), preferred_element_type=jnp.float32)
        .astype(jnp.bfloat16)
        .reshape(row_count, state_dim, channels)
    )
    moved_conv = (
        jnp.dot(place_hot, recv_conv.reshape(slot_count, -1), preferred_element_type=jnp.float32)
        .astype(jnp.bfloat16)
        .reshape(row_count, -1, channels)
    )
    window = jnp.concatenate([moved_conv, conv_input[:, None, :]], axis=1)
    conv_new = window[:, 1:, :]
    conv_sum = (
        jnp.sum(window.astype(jnp.float32) * conv_weight[None, :, :], axis=1) + conv_bias[None, :]
    )
    activated = jax.nn.silu(conv_sum).astype(jnp.bfloat16)
    projected = dp_total(jnp.dot(activated, x_proj_weight, preferred_element_type=jnp.float32))
    rank_dim = step_weight.shape[0]
    step_low = projected[:, :rank_dim]
    b_coef = projected[:, rank_dim : rank_dim + state_dim]
    c_coef = projected[:, rank_dim + state_dim :]
    step_norm = (
        step_low * lax.rsqrt(jnp.mean(step_low * step_low, axis=1, keepdims=True) + 1e-06)
    ).astype(jnp.bfloat16)
    step_size = jax.nn.softplus(
        jnp.dot(step_norm, step_weight, preferred_element_type=jnp.float32) + step_bias[None, :]
    )
    act_float = activated.astype(jnp.float32)
    decays = jnp.exp(step_size[:, None, :] * (-jnp.exp(decay_log))[None, :, :])
    states = (
        decays * moved_ssm.astype(jnp.float32)
        + (step_size * act_float)[:, None, :] * b_coef[:, :, None]
    )
    ssm_new = states.astype(jnp.bfloat16)
    gated_out = (
        (jnp.sum(c_coef[:, :, None] * states, axis=1) + skip_gain[None, :] * act_float)
        * jax.nn.silu(gate_input.astype(jnp.float32))
    ).astype(jnp.bfloat16)
    mamba_mix = dp_total(
        jnp.dot(
            lax.all_gather(gated_out, "expert", axis=0, tiled=True),
            out_proj_weight,
            preferred_element_type=jnp.float32,
        )
    )
    stream = (residual.astype(jnp.float32) + mamba_mix).astype(jnp.bfloat16)
    top_count = routes.shape[1]
    width = stream.shape[1]
    capacity = min(row_count, 5 * row_count * top_count // (2 * owners))
    expert_hot = (
        (routes[:, :, None] == jnp.arange(owners)[None, None, :])
        .astype(jnp.int32)
        .reshape(owners, row_count * top_count, owners)
    )
    prior = jnp.sum((jnp.cumsum(expert_hot, axis=1) - expert_hot) * expert_hot, axis=2)
    slot_of = (routes.reshape(owners, row_count * top_count) * capacity + prior).reshape(
        owners, row_count, top_count
    )
    matches = slot_of[:, :, :, None] == jnp.arange(owners * capacity)[None, None, None, :]
    dispatch_hot = (
        jnp.any(matches, axis=2).astype(jnp.bfloat16).reshape(owners, row_count, owners, capacity)
    )
    combine_w = jnp.sum(
        jnp.where(matches, gate_weight.reshape(owners, row_count, top_count)[:, :, :, None], 0.0),
        axis=2,
    ).reshape(owners, row_count, owners, capacity)
    outgoing = jnp.einsum(
        "orec,ord->eocd",
        dispatch_hot,
        stream.reshape(owners, row_count, width),
        preferred_element_type=jnp.float32,
    ).astype(jnp.bfloat16)
    arrived = lax.all_to_all(outgoing, "expert", split_axis=0, concat_axis=3, tiled=True)
    tokens = arrived.reshape(owners * capacity, -1).astype(jnp.float32)
    normed = (
        tokens
        * lax.rsqrt(jnp.mean(tokens * tokens, axis=1, keepdims=True) + 1e-05)
        * norm_gain[None, :]
    ).astype(jnp.bfloat16)
    gate_val = jnp.dot(normed, expert_gate[0], preferred_element_type=jnp.float32)
    up_val = jnp.dot(normed, expert_up[0], preferred_element_type=jnp.float32)
    hidden = (jax.nn.silu(gate_val) * up_val).astype(jnp.bfloat16)
    partial_out = jnp.dot(hidden, expert_down[0], preferred_element_type=jnp.float32).reshape(
        owners, capacity, -1
    )
    summed = dp_total(partial_out)
    returned = lax.all_to_all(
        summed.astype(jnp.bfloat16), "expert", split_axis=2, concat_axis=0, tiled=True
    ).astype(summed.dtype)
    expert_mix = jnp.einsum(
        "orec,eocd->ord",
        combine_w,
        returned.reshape(owners, owners, capacity, width),
        precision=lax.Precision.HIGHEST,
        preferred_element_type=jnp.float32,
    )
    layer_out = (stream.astype(jnp.float32) + expert_mix.reshape(-1, width)).astype(jnp.bfloat16)
    return (ssm_new, conv_new, layer_out)


def solution(mesh):
    in_specs = (
        P("expert", None, "dp"),
        P("expert", None, "dp"),
        P(),
        P("expert", "dp"),
        P("expert", "dp"),
        P(None, "dp"),
        P("dp"),
        P("dp", None),
        P(None, "dp"),
        P("dp"),
        P(None, "dp"),
        P("dp"),
        P("dp", "expert"),
        P(None, "expert"),
        P(),
        P(),
        P(),
        P("expert", None, "dp"),
        P("expert", None, "dp"),
        P("expert", "dp", None),
    )
    out_specs = (P("expert", None, "dp"), P("expert", None, "dp"), P(None, "expert"))
    return jax.shard_map(body, mesh=mesh, in_specs=in_specs, out_specs=out_specs, check_vma=False)
```

profile of v0, /device:TPU:97, one launch (start us, length us, event | category | flops | bytes accessed | tf_op | source)
XLA Modules:
  0.0 587.0 jit_solution(9232045870672755872)
XLA Ops:
  7.2 0.8 and_select_fusion
  8.1 0.1 reduce_window_sum.37
  8.2 0.2 select_reduce_fusion.2
  8.4 0.8 multiply_add_fusion
  9.1 0.9 copy.107
  10.0 0.9 fusion.30
  10.9 6.9 %all-to-all-start = ((bf16[16,8,768]{2,1,0:T(8,128)(2,1)}), bf16[16,8,768]{2,1,0:T(8,128)(2,1)S(1)}, u32[]{:S(2)}, u32[]{:S(2)}) async-start(bf16[16,8,768]{2,1,0:T(8,128)(2,1)} %fusion.30), calls=%async_computation | async-start | bytes 393216 | tf_op jit(solution)/shard_map/all_to_all | solution.py:56
  17.8 0.7 broadcast_compare_fusion
  18.6 0.2 reduce_window_sum.35
  18.9 0.7 add_select_fusion.2
  19.6 1.3 copy.108
  20.9 1.4 fusion.3
  22.3 0.4 convolution_convert_fusion.4
  22.7 2.3 all-to-all-done
  25.0 4.4 all-to-all-start.1
  29.4 0.2 convolution_convert_fusion.3
  29.6 0.3 multiply_reduce_fusion.1
  29.9 0.8 fusion.63
  30.9 108.3 %all-reduce.4.cloned.1.call-done = f32[64,288]{1,0:T(8,128)} async-done(((f32[64,288]{1,0:T(8,128)}), f32[64,288]{1,0:T(8,128)}) %all-reduce.4.cloned.1.call-update) | async-done | bytes 73744 | tf_op jit(solution)/shard_map/psum | solution.py:8
  139.2 0.9 multiply_reduce_fusion.2
  140.2 0.9 fusion.65
  141.1 1.1 convert_multiply_fusion.4
  142.2 0.3 fusion.4
  142.5 0.3 copy.109
  142.9 1.3 multiply_reduce_fusion
  144.2 19.4 %all_gather.3 = bf16[1024,256]{1,0:T(8,128)(2,1)S(1)} all-gather(bf16[64,256]{1,0:T(8,128)(2,1)S(1)} %fusion.46), channel_id=1, replica_groups=mesh['dp'=16,'expert'=16] {'expert'}, dimensions={0}, use_global_device_ids=true | all-gather | bytes 557056 | tf_op jit(solution)/shard_map/all_gather | solution.py:111
  163.6 1.3 fusion.66
  165.0 0.2 copy.85
  165.2 0.1 mul.175
  165.3 0.3 eq.109
  165.5 0.1 copy.86
  165.7 2.8 select_reduce_fusion.1
  168.6 0.7 fusion.11
  169.2 1.3 copy.91
  170.6 109.3 %all-reduce.6.cloned.1.call-done = f32[1024,256]{1,0:T(8,128)} async-done(((f32[1024,256]{1,0:T(8,128)}), f32[1024,256]{1,0:T(8,128)}) %all-reduce.6.cloned.1.call-update) | async-done | bytes 1048592 | tf_op jit(solution)/shard_map/psum | solution.py:8
  279.8 1.3 add_convert_fusion
  281.2 1.0 convert_bitcast_fusion
  282.1 3.0 copy.93
  285.1 6.7 %all-to-all-start.2 = ((bf16[16,16,20,256]{3,1,2,0:T(8,128)(2,1)}), bf16[16,16,20,256]{3,1,2,0:T(8,128)(2,1)S(1)}, u32[]{:S(2)}, u32[]{:S(2)}) async-start(bf16[16,16,20,256]{3,1,2,0:T(8,128)(2,1)} %copy.93), calls=%async_computation.2 | async-start | bytes 5242880 | tf_op jit(solution)/shard_map/all_to_all | solution.py:143
  291.8 41.7 %all-to-all-done.2 = bf16[16,16,20,256]{3,1,2,0:T(8,128)(2,1)S(1)} async-done(((bf16[16,16,20,256]{3,1,2,0:T(8,128)(2,1)}), bf16[16,16,20,256]{3,1,2,0:T(8,128)(2,1)S(1)}, u32[]{:S(2)}, u32[]{:S(2)}) %all-to-all-start.2) | async-done | bytes 2621472 | tf_op jit(solution)/shard_map/all_to_all | solution.py:143
  333.6 0.6 fusion
  334.1 0.8 fusion.14
  334.9 1.5 copy.94
  336.4 1.2 copy.110
  337.6 0.8 copy-done.13
  338.4 1.5 fusion.9
  340.0 0.5 copy-done.14
  340.5 1.5 fusion.27
  342.0 0.1 dot_general.52
  342.1 5.9 %fusion.5 = f32[16,20,4096]{2,0,1:T(8,128)} fusion(bf16[1,448,4096]{2,1,0:T(8,128)(2,1)} %param.39, bf16[16,20,448]{2,1,0:T(8,128)(2,1)S(1)} %dot_general.52), kind=kOutput, calls=%fused_computation.9 | convolution fusion | flops 1174405120 | bytes 9199616 | tf_op jit(solution)/shard_map/dot_general | solution.py:153
  348.0 74.7 %all-reduce.7 = bf16[16,20,4096]{2,0,1:T(8,128)(2,1)S(1)} all-reduce(f32[16,20,4096]{2,0,1:T(8,128)} %fusion.5), channel_id=1, replica_groups=mesh['dp'=16,'expert'=16] {'dp'}, use_global_device_ids=true, to_apply=%region_13.14 | all-reduce | flops 1310720 | bytes 7864320 | tf_op jit(solution)/shard_map/psum | solution.py:8
  422.7 14.9 %copy.96 = bf16[16,20,4096]{1,0,2:T(8,128)(2,1)} copy(bf16[16,20,4096]{2,0,1:T(8,128)(2,1)S(1)} %all-reduce.7) | data formatting | bytes 5242880 | tf_op jit(solution)/shard_map/convert_element_type | solution.py:158
  437.6 34.7 %reshape.150 = bf16[16,2,40960]{2,1,0:T(2,128)(2,1)} reshape(bf16[4096,16,20]{2,1,0:T(8,128)(2,1)} %bitcast.85) | data formatting | bytes 5242880
  472.3 4.1 all-to-all-start.3
  476.4 0.1 broadcast_in_dim.13
  476.5 2.0 select_reduce_fusion
  478.5 3.1 copy.90
  481.6 0.2 fusion.41
  481.8 0.7 copy.100
  482.4 35.1 %all-to-all-done.3 = bf16[16,2,40960]{2,1,0:T(2,128)(2,1)S(1)} async-done(((bf16[16,2,40960]{2,1,0:T(2,128)(2,1)}), bf16[16,2,40960]{2,1,0:T(2,128)(2,1)S(1)}, u32[]{:S(2)}, u32[]{:S(2)}) %all-to-all-start.3) | async-done | bytes 2621472 | tf_op jit(solution)/shard_map/all_to_all | solution.py:157
  517.5 42.4 %reshape.151 = bf16[4096,16,20]{2,1,0:T(8,128)(2,1)} reshape(bf16[16,2,40960]{2,1,0:T(2,128)(2,1)S(1)} %all-to-all-done.3) | data formatting | bytes 5242880
  559.9 14.0 %copy.98 = bf16[16,20,16,256]{3,2,1,0:T(8,128)(2,1)S(1)} copy(bf16[16,20,16,256]{1,0,3,2:T(8,128)(2,1)} %bitcast.86) | data formatting | bytes 5242880 | tf_op jit(solution)/shard_map/all_to_all | solution.py:157
  573.9 5.3 fusion.15
  579.2 0.9 fusion.32
  (52 shorter events, 0.7 us)
Async XLA Ops:
  7.2 22.8 %copy-start = (bf16[256,288]{0,1:T(8,128)(2,1)S(1)}, bf16[256,288]{0,1:T(8,128)(2,1)}, u32[]{:S(2)}) copy-start(bf16[256,288]{0,1:T(8,128)(2,1)} %param.27) | copy-start | bytes 442372
  7.2 15.1 %copy-start.5 = (bf16[64,256]{1,0:T(8,128)(2,1)S(1)}, bf16[64,256]{1,0:T(8,128)(2,1)}, u32[]{:S(2)}) copy-start(bf16[64,256]{1,0:T(8,128)(2,1)} %param.23) | copy-start | bytes 98308
  10.9 18.7 %copy-start.10 = (f32[4,256]{1,0:T(4,128)S(1)}, f32[4,256]{1,0:T(4,128)}, u32[]{:S(2)}) copy-start(f32[4,256]{1,0:T(4,128)} %param.25) | copy-start | bytes 12292
  10.9 19.0 %copy-start.11 = (f32[256]{0:T(256)S(1)}, f32[256]{0:T(256)}, u32[]{:S(2)}) copy-start(f32[256]{0:T(256)} %param.26) | copy-start | bytes 3076
  10.9 14.1 %all-to-all-start = ((bf16[16,8,768]{2,1,0:T(8,128)(2,1)}), bf16[16,8,768]{2,1,0:T(8,128)(2,1)S(1)}, u32[]{:S(2)}, u32[]{:S(2)}) async-start(bf16[16,8,768]{2,1,0:T(8,128)(2,1)} %fusion.30), calls=%async_computation | async-start | bytes 393216 | tf_op jit(solution)/shard_map/all_to_all | solution.py:56
  19.6 11.3 %copy-start.7 = (f32[16,256]{1,0:T(8,128)S(1)}, f32[16,256]{1,0:T(8,128)}, u32[]{:S(2)}) copy-start(f32[16,256]{1,0:T(8,128)} %param.30) | copy-start | bytes 49156
  19.6 121.5 %copy-start.15 = (bf16[256,256]{1,0:T(8,128)(2,1)S(1)}, bf16[256,256]{1,0:T(8,128)(2,1)}, u32[]{:S(2)}) copy-start(bf16[256,256]{1,0:T(8,128)(2,1)} %param.28) | copy-start | bytes 393220
  19.6 121.5 %copy-start.16 = (f32[256]{0:T(256)S(1)}, f32[256]{0:T(256)}, u32[]{:S(2)}) copy-start(f32[256]{0:T(256)} %param.29) | copy-start | bytes 3076
  25.0 117.2 %all-to-all-start.1 = ((bf16[16,8,4096]{2,1,0:T(8,128)(2,1)}), bf16[16,8,4096]{2,1,0:T(8,128)(2,1)S(1)}, u32[]{:S(2)}, u32[]{:S(2)}) async-start(bf16[16,8,4096]{2,1,0:T(8,128)(2,1)} %fusion.3), calls=%async_computation.1 | async-start | bytes 2097152 | tf_op jit(solution)/shard_map/all_to_all | solution.py:55
  29.4 109.9 %all-reduce.4.cloned.1.call-start = ((), (), s32[]{:S(2)}) async-start(), calls=%async_computation.4 | async-start | bytes 196608 | tf_op jit(solution)/shard_map/psum | solution.py:8
  30.8 249.0 %all-reduce.6.cloned.1.call-start = ((), (), s32[]{:S(2)}) async-start(), calls=%async_computation.5 | async-start | bytes 2097152 | tf_op jit(solution)/shard_map/psum | solution.py:8
  142.2 2.0 copy-start.6
  142.2 2.0 copy-start.12
  142.2 21.4 %copy-start.3 = (bf16[256,256]{1,0:T(8,128)(2,1)S(1)}, bf16[256,256]{1,0:T(8,128)(2,1)}, u32[]{:S(2)}) copy-start(bf16[256,256]{1,0:T(8,128)(2,1)} %param.32) | copy-start | bytes 393220
  142.8 22.1 %copy-start.4 = (s32[1024,2]{0,1:T(2,128)S(1)}, s32[1024,2]{0,1:T(2,128)}, u32[]{:S(2)}) copy-start(s32[1024,2]{0,1:T(2,128)} %param.35) | copy-start | bytes 24580
  144.2 135.6 %copy-start.2 = (bf16[1024,256]{1,0:T(8,128)(2,1)S(1)}, bf16[1024,256]{1,0:T(8,128)(2,1)}, u32[]{:S(2)}) copy-start(bf16[1024,256]{1,0:T(8,128)(2,1)} %param.33) | copy-start | bytes 1572868
  285.1 6.7 %copy-start.8 = (f32[4096]{0:T(1024)S(1)}, f32[4096]{0:T(1024)}, u32[]{:S(2)}) copy-start(f32[4096]{0:T(1024)} %param.34) | copy-start | bytes 49156
  285.1 48.4 %all-to-all-start.2 = ((bf16[16,16,20,256]{3,1,2,0:T(8,128)(2,1)}), bf16[16,16,20,256]{3,1,2,0:T(8,128)(2,1)S(1)}, u32[]{:S(2)}, u32[]{:S(2)}) async-start(bf16[16,16,20,256]{3,1,2,0:T(8,128)(2,1)} %copy.93), calls=%async_computation.2 | async-start | bytes 5242880 | tf_op jit(solution)/shard_map/all_to_all | solution.py:143
  336.4 2.0 copy-start.13
  338.4 2.0 copy-start.14
  472.3 4.1 copy-start.9
  472.3 45.2 %all-to-all-start.3 = ((bf16[16,2,40960]{2,1,0:T(2,128)(2,1)}), bf16[16,2,40960]{2,1,0:T(2,128)(2,1)S(1)}, u32[]{:S(2)}, u32[]{:S(2)}) async-start(bf16[16,2,40960]{2,1,0:T(2,128)(2,1)} %reshape.150), calls=%async_computation.3 | async-start | bytes 5242880 | tf_op jit(solution)/shard_map/all_to_all | solution.py:157
  573.9 6.2 %copy-start.1 = (bf16[256,288]{0,1:T(8,128)(2,1)S(1)}, bf16[256,288]{0,1:T(8,128)(2,1)}, u32[]{:S(2)}) copy-start(bf16[256,288]{0,1:T(8,128)(2,1)} %param.27) | copy-start | bytes 442372
Sparse Core Ops, SparseCore 0:
  33.1 106.0 all-reduce.3
  165.1 114.7 all-reduce.5
where the time goes:
time: 588 us; the launch traced here: 587 us
  waiting for transfers between devices  297 us (51%)
  local copies, waits for them, and re-layouts  123 us (21%)
  blocking collectives  94 us (16%)
  starting transfers between devices  22.1 us (4%)
  matrix products  21.5 us (4%)
  other arithmetic  15.4 us (3%)
  between operations  14.5 us (2%)
    psum x2, waiting for transfers between devices, dp_total(): return lax.psum(values, 'dp')  218 us
    unnamed x41, local copies, waits for them, and re-layouts  82.2 us
    psum x1, blocking collectives, dp_total(): return lax.psum(values, 'dp')  74.7 us
    all_to_all x1, waiting for transfers between devices, body(): lax.all_to_all(outgoing, 'expert', split_axis=0, concat_axis=3, tiled=True)  41.7 us
    all_to_all x1, waiting for transfers between devices, body(): lax.all_to_all(summed.astype(jnp.bfloat16), 'expert', split_axis=2, conca...  35.1 us
    all_gather x1, blocking collectives, body(): lax.all_gather(gated_out, 'expert', axis=0, tiled=True)  19.4 us
    convert_element_type x1, local copies, waits for them, and re-layouts, body(): summed.astype(jnp.bfloat16)  14.9 us
    all_to_all x1, local copies, waits for them, and re-layouts, body(): lax.all_to_all(summed.astype(jnp.bfloat16), 'expert', split_axis=2, conca...  14 us
  transfers between devices with their start and end apart: 6, of which 5 were waited for; matrix products, arithmetic and copies ran while one was open for 4% of the time, Pallas kernels for 0%

commit v1 on v0

--- a/solution.py
+++ b/solution.py
@@ -140,7 +140,11 @@
         stream.reshape(owners, row_count, width),
         preferred_element_type=jnp.float32,
     ).astype(jnp.bfloat16)
-    arrived = lax.all_to_all(outgoing, "expert", split_axis=0, concat_axis=3, tiled=True)
+    reply = jax.lax.axis_size("expert")
+    extra = jnp.split(outgoing, reply, 0)
+    oldest = jnp.stack(extra, 0)
+    r2 = jax.lax.all_to_all(oldest, axis_name="expert", split_axis=0, concat_axis=0)
+    arrived = jnp.concatenate(r2, axis=3)
     tokens = arrived.reshape(owners * capacity, -1).astype(jnp.float32)
     normed = (
         tokens

time: 588 us -> 588 us (level)
    unnamed x41 -> x56, local copies, waits for them, and re-layouts: 82.2 us -> 82.4 us
where the time goes in v1:
time: 588 us; the launch traced here: 587 us
  waiting for transfers between devices  297 us (51%)
  local copies, waits for them, and re-layouts  122 us (21%)
  blocking collectives  94 us (16%)
  starting transfers between devices  22.1 us (4%)
  matrix products  21.5 us (4%)
  other arithmetic  15.4 us (3%)
  between operations  14.6 us (2%)
    psum x2, waiting for transfers between devices, dp_total(): return lax.psum(values, 'dp')  218 us
    unnamed x56, local copies, waits for them, and re-layouts  82.4 us
    psum x1, blocking collectives, dp_total(): return lax.psum(values, 'dp')  74.7 us
    all_to_all x1, waiting for transfers between devices, body(): jax.lax.all_to_all(oldest, axis_name='expert', split_axis=0, concat_axis=0)  41.7 us
    all_to_all x1, waiting for transfers between devices, body(): lax.all_to_all(summed.astype(jnp.bfloat16), 'expert', split_axis=2, conca...  35.1 us
    all_gather x1, blocking collectives, body(): lax.all_gather(gated_out, 'expert', axis=0, tiled=True)  19.4 us
    convert_element_type x1, local copies, waits for them, and re-layouts, body(): summed.astype(jnp.bfloat16)  14.9 us
    all_to_all x1, local copies, waits for them, and re-layouts, body(): lax.all_to_all(summed.astype(jnp.bfloat16), 'expert', split_axis=2, conca...  14 us
  transfers between devices with their start and end apart: 6, of which 5 were waited for; matrix products, arithmetic and copies ran while one was open for 4% of the time, Pallas kernels for 0%

profile of v1, /device:TPU:97, one launch (start us, length us, event | category | flops | bytes accessed | tf_op | source)
XLA Modules:
  0.0 586.7 jit_solution(7184945800215089622)
XLA Ops:
  7.2 0.8 and_select_fusion
  8.1 0.1 reduce_window_sum.37
  8.2 0.2 select_reduce_fusion.2
  8.4 0.8 multiply_add_fusion
  9.1 0.9 copy.212
  10.0 0.9 fusion.30
  10.9 6.9 %all-to-all-start = ((bf16[16,8,768]{2,1,0:T(8,128)(2,1)}), bf16[16,8,768]{2,1,0:T(8,128)(2,1)S(1)}, u32[]{:S(2)}, u32[]{:S(2)}) async-start(bf16[16,8,768]{2,1,0:T(8,128)(2,1)} %fusion.30), calls=%async_computation | async-start | bytes 393216 | tf_op jit(solution)/shard_map/all_to_all | solution.py:56
  17.8 0.7 broadcast_compare_fusion
  18.6 0.2 reduce_window_sum.35
  18.9 0.7 add_select_fusion.2
  19.6 1.3 copy.213
  20.9 1.4 fusion.3
  22.3 0.4 convolution_convert_fusion.4
  22.7 2.3 all-to-all-done
  25.0 4.4 all-to-all-start.1
  29.4 0.2 convolution_convert_fusion.3
  29.6 0.3 multiply_reduce_fusion.1
  29.9 0.8 fusion.79
  30.9 108.3 %all-reduce.4.cloned.1.call-done = f32[64,288]{1,0:T(8,128)} async-done(((f32[64,288]{1,0:T(8,128)}), f32[64,288]{1,0:T(8,128)}) %all-reduce.4.cloned.1.call-update) | async-done | bytes 73744 | tf_op jit(solution)/shard_map/psum | solution.py:8
  139.2 0.9 multiply_reduce_fusion.2
  140.2 0.9 fusion.81
  141.1 1.1 convert_multiply_fusion.4
  142.2 0.3 fusion.4
  142.5 0.3 copy.214
  142.9 1.3 multiply_reduce_fusion
  144.2 19.4 %all_gather.3 = bf16[1024,256]{1,0:T(8,128)(2,1)S(1)} all-gather(bf16[64,256]{1,0:T(8,128)(2,1)S(1)} %fusion.62), channel_id=1, replica_groups=mesh['dp'=16,'expert'=16] {'expert'}, dimensions={0}, use_global_device_ids=true | all-gather | bytes 557056 | tf_op jit(solution)/shard_map/all_gather | solution.py:111
  163.6 1.3 fusion.82
  165.0 0.2 copy.160
  165.2 0.1 mul.175
  165.3 0.3 eq.109
  165.5 0.1 copy.161
  165.7 2.8 select_reduce_fusion.1
  168.6 0.7 fusion.11
  169.2 1.3 copy.166
  170.6 109.3 %all-reduce.6.cloned.1.call-done = f32[1024,256]{1,0:T(8,128)} async-done(((f32[1024,256]{1,0:T(8,128)}), f32[1024,256]{1,0:T(8,128)}) %all-reduce.6.cloned.1.call-update) | async-done | bytes 1048592 | tf_op jit(solution)/shard_map/psum | solution.py:8
  279.8 1.3 add_convert_fusion
  281.2 1.0 convert_bitcast_fusion
  282.6 2.2 copy.183
  284.8 6.7 %all-to-all-start.2 = ((bf16[16,1,16,20,256]{4,2,3,1,0:T(8,128)(2,1)}), bf16[16,1,16,20,256]{4,2,3,1,0:T(8,128)(2,1)S(1)}, u32[]{:S(2)}, u32[]{:S(2)}) async-start(bf16[16,1,16,20,256]{4,2,3,1,0:T(8,128)(2,1)} %copy.183), calls=%async_computation.2 | async-start | bytes 5242880 | tf_op jit(solution)/shard_map/all_to_all | solution.py:146
  291.5 41.7 %all-to-all-done.2 = bf16[16,1,16,20,256]{4,2,3,1,0:T(8,128)(2,1)S(1)} async-done(((bf16[16,1,16,20,256]{4,2,3,1,0:T(8,128)(2,1)}), bf16[16,1,16,20,256]{4,2,3,1,0:T(8,128)(2,1)S(1)}, u32[]{:S(2)}, u32[]{:S(2)}) %all-to-all-start.2) | async-done | bytes 2621472 | tf_op jit(solution)/shard_map/all_to_all | solution.py:146
  333.2 0.6 fusion
  333.8 0.8 fusion.14
  334.6 1.5 copy.184
  336.1 1.2 copy.215
  337.3 0.8 copy-done.13
  338.1 1.5 fusion.9
  339.6 0.5 copy-done.14
  340.1 1.5 fusion.27
  341.7 0.1 dot_general.52
  341.8 5.9 %fusion.5 = f32[16,20,4096]{2,0,1:T(8,128)} fusion(bf16[1,448,4096]{2,1,0:T(8,128)(2,1)} %param.39, bf16[16,20,448]{2,1,0:T(8,128)(2,1)S(1)} %dot_general.52), kind=kOutput, calls=%fused_computation.9 | convolution fusion | flops 1174405120 | bytes 9199616 | tf_op jit(solution)/shard_map/dot_general | solution.py:157
  347.7 74.7 %all-reduce.7 = bf16[16,20,4096]{2,0,1:T(8,128)(2,1)S(1)} all-reduce(f32[16,20,4096]{2,0,1:T(8,128)} %fusion.5), channel_id=1, replica_groups=mesh['dp'=16,'expert'=16] {'dp'}, use_global_device_ids=true, to_apply=%region_13.14 | all-reduce | flops 1310720 | bytes 7864320 | tf_op jit(solution)/shard_map/psum | solution.py:8
  422.4 14.9 %copy.186 = bf16[16,20,4096]{1,0,2:T(8,128)(2,1)} copy(bf16[16,20,4096]{2,0,1:T(8,128)(2,1)S(1)} %all-reduce.7) | data formatting | bytes 5242880 | tf_op jit(solution)/shard_map/convert_element_type | solution.py:162
  437.2 34.7 %reshape.146 = bf16[16,2,40960]{2,1,0:T(2,128)(2,1)} reshape(bf16[4096,16,20]{2,1,0:T(8,128)(2,1)} %bitcast.175) | data formatting | bytes 5242880
  471.9 4.1 all-to-all-start.3
  476.1 0.1 broadcast_in_dim.13
  476.2 2.0 select_reduce_fusion
  478.1 3.1 copy.165
  481.3 0.2 fusion.57
  481.4 0.7 copy.190
  482.1 35.1 %all-to-all-done.3 = bf16[16,2,40960]{2,1,0:T(2,128)(2,1)S(1)} async-done(((bf16[16,2,40960]{2,1,0:T(2,128)(2,1)}), bf16[16,2,40960]{2,1,0:T(2,128)(2,1)S(1)}, u32[]{:S(2)}, u32[]{:S(2)}) %all-to-all-start.3) | async-done | bytes 2621472 | tf_op jit(solution)/shard_map/all_to_all | solution.py:161
  517.2 42.4 %reshape.147 = bf16[4096,16,20]{2,1,0:T(8,128)(2,1)} reshape(bf16[16,2,40960]{2,1,0:T(2,128)(2,1)S(1)} %all-to-all-done.3) | data formatting | bytes 5242880
  559.6 14.0 %copy.188 = bf16[16,20,16,256]{3,2,1,0:T(8,128)(2,1)S(1)} copy(bf16[16,20,16,256]{1,0,3,2:T(8,128)(2,1)} %bitcast.176) | data formatting | bytes 5242880 | tf_op jit(solution)/shard_map/all_to_all | solution.py:161
  573.6 5.3 fusion.15
  578.9 0.9 fusion.32
  (68 shorter events, 1.0 us)
Async XLA Ops:
  7.2 22.8 %copy-start = (bf16[256,288]{0,1:T(8,128)(2,1)S(1)}, bf16[256,288]{0,1:T(8,128)(2,1)}, u32[]{:S(2)}) copy-start(bf16[256,288]{0,1:T(8,128)(2,1)} %param.27) | copy-start | bytes 442372
  7.2 15.1 %copy-start.5 = (bf16[64,256]{1,0:T(8,128)(2,1)S(1)}, bf16[64,256]{1,0:T(8,128)(2,1)}, u32[]{:S(2)}) copy-start(bf16[64,256]{1,0:T(8,128)(2,1)} %param.23) | copy-start | bytes 98308
  10.9 18.7 %copy-start.10 = (f32[4,256]{1,0:T(4,128)S(1)}, f32[4,256]{1,0:T(4,128)}, u32[]{:S(2)}) copy-start(f32[4,256]{1,0:T(4,128)} %param.25) | copy-start | bytes 12292
  10.9 19.0 %copy-start.11 = (f32[256]{0:T(256)S(1)}, f32[256]{0:T(256)}, u32[]{:S(2)}) copy-start(f32[256]{0:T(256)} %param.26) | copy-start | bytes 3076
  10.9 14.1 %all-to-all-start = ((bf16[16,8,768]{2,1,0:T(8,128)(2,1)}), bf16[16,8,768]{2,1,0:T(8,128)(2,1)S(1)}, u32[]{:S(2)}, u32[]{:S(2)}) async-start(bf16[16,8,768]{2,1,0:T(8,128)(2,1)} %fusion.30), calls=%async_computation | async-start | bytes 393216 | tf_op jit(solution)/shard_map/all_to_all | solution.py:56
  19.6 11.3 %copy-start.7 = (f32[16,256]{1,0:T(8,128)S(1)}, f32[16,256]{1,0:T(8,128)}, u32[]{:S(2)}) copy-start(f32[16,256]{1,0:T(8,128)} %param.30) | copy-start | bytes 49156
  19.6 121.5 %copy-start.15 = (bf16[256,256]{1,0:T(8,128)(2,1)S(1)}, bf16[256,256]{1,0:T(8,128)(2,1)}, u32[]{:S(2)}) copy-start(bf16[256,256]{1,0:T(8,128)(2,1)} %param.28) | copy-start | bytes 393220
  19.6 121.5 %copy-start.16 = (f32[256]{0:T(256)S(1)}, f32[256]{0:T(256)}, u32[]{:S(2)}) copy-start(f32[256]{0:T(256)} %param.29) | copy-start | bytes 3076
  25.0 117.2 %all-to-all-start.1 = ((bf16[16,8,4096]{2,1,0:T(8,128)(2,1)}), bf16[16,8,4096]{2,1,0:T(8,128)(2,1)S(1)}, u32[]{:S(2)}, u32[]{:S(2)}) async-start(bf16[16,8,4096]{2,1,0:T(8,128)(2,1)} %fusion.3), calls=%async_computation.1 | async-start | bytes 2097152 | tf_op jit(solution)/shard_map/all_to_all | solution.py:55
  29.4 109.9 %all-reduce.4.cloned.1.call-start = ((), (), s32[]{:S(2)}) async-start(), calls=%async_computation.4 | async-start | bytes 196608 | tf_op jit(solution)/shard_map/psum | solution.py:8
  30.8 249.0 %all-reduce.6.cloned.1.call-start = ((), (), s32[]{:S(2)}) async-start(), calls=%async_computation.5 | async-start | bytes 2097152 | tf_op jit(solution)/shard_map/psum | solution.py:8
  142.2 2.0 copy-start.6
  142.2 2.0 copy-start.12
  142.2 21.4 %copy-start.3 = (bf16[256,256]{1,0:T(8,128)(2,1)S(1)}, bf16[256,256]{1,0:T(8,128)(2,1)}, u32[]{:S(2)}) copy-start(bf16[256,256]{1,0:T(8,128)(2,1)} %param.32) | copy-start | bytes 393220
  142.8 22.1 %copy-start.4 = (s32[1024,2]{0,1:T(2,128)S(1)}, s32[1024,2]{0,1:T(2,128)}, u32[]{:S(2)}) copy-start(s32[1024,2]{0,1:T(2,128)} %param.35) | copy-start | bytes 24580
  144.2 135.6 %copy-start.2 = (bf16[1024,256]{1,0:T(8,128)(2,1)S(1)}, bf16[1024,256]{1,0:T(8,128)(2,1)}, u32[]{:S(2)}) copy-start(bf16[1024,256]{1,0:T(8,128)(2,1)} %param.33) | copy-start | bytes 1572868
  284.8 6.7 %copy-start.8 = (f32[4096]{0:T(1024)S(1)}, f32[4096]{0:T(1024)}, u32[]{:S(2)}) copy-start(f32[4096]{0:T(1024)} %param.34) | copy-start | bytes 49156
  284.8 48.4 %all-to-all-start.2 = ((bf16[16,1,16,20,256]{4,2,3,1,0:T(8,128)(2,1)}), bf16[16,1,16,20,256]{4,2,3,1,0:T(8,128)(2,1)S(1)}, u32[]{:S(2)}, u32[]{:S(2)}) async-start(bf16[16,1,16,20,256]{4,2,3,1,0:T(8,128)(2,1)} %copy.183), calls=%async_computation.2 | async-start | bytes 5242880 | tf_op jit(solution)/shard_map/all_to_all | solution.py:146
  336.1 2.0 copy-start.13
  338.1 2.0 copy-start.14
  471.9 4.1 copy-start.9
  471.9 45.2 %all-to-all-start.3 = ((bf16[16,2,40960]{2,1,0:T(2,128)(2,1)}), bf16[16,2,40960]{2,1,0:T(2,128)(2,1)S(1)}, u32[]{:S(2)}, u32[]{:S(2)}) async-start(bf16[16,2,40960]{2,1,0:T(2,128)(2,1)} %reshape.146), calls=%async_computation.3 | async-start | bytes 5242880 | tf_op jit(solution)/shard_map/all_to_all | solution.py:161
  573.6 6.2 %copy-start.1 = (bf16[256,288]{0,1:T(8,128)(2,1)S(1)}, bf16[256,288]{0,1:T(8,128)(2,1)}, u32[]{:S(2)}) copy-start(bf16[256,288]{0,1:T(8,128)(2,1)} %param.27) | copy-start | bytes 442372
Sparse Core Ops, SparseCore 0:
  33.1 106.0 all-reduce.3
  165.1 114.7 all-reduce.5
